TPU v7x, 128 devices: a whole 4x4x4 slice. The times are simulated.
128 devices in a mesh: row: 8 (over y_hi, z), col: 16 (over y_lo, x, core).
Axes of the slice: x: 4, y: 4 (y_hi: 2, y_lo: 2; y = y_hi * 2 + y_lo), z: 4, core: 2. Of those that a mesh axis runs over, the one named last changes fastest.
Arguments:
- a_tiles: float32 [8, 16, 8, 128, 128], P('row', 'col'), may hold values from -6 to 6
- b_tiles: float32 [8, 16, 8, 128, 128], P('row', 'col'), may hold values from -0.25 to 0.25
- pair_lists: int32 [8, 16, 16, 3, 32], P('row', 'col'), may hold values from 0 to 63, as said below
- stack_counts: int32 [8, 16, 16], P('row', 'col'), may hold values from 1 to 32, as said below
Outputs:
- c_tiles: float32 [8, 16, 32, 128, 128], P('row', 'col')
Inputs may be any that keep to these rules, and one draw needn't show every extreme that they name: `pair_lists`: entry 0 of a list column is an A tile slot below 8, entry 1 a tile of bcol below 64, entry 2 a product tile below 32; entries past the live count are valid indices that do not count. `stack_counts`: live entries of each list; in every draw some list has all 32 live.
All inputs are finite; a program needn't handle non-finite values.
Results may differ from a plain program's by a relative error of at most 0.0003.
Values sent between devices are 32-bit elements; how exact they have to be, the bound alone decides.
No kernel may reach another device: no remote copies, remote signals or barrier semaphores. Data moves between devices by JAX's collectives and lax.ppermute only.
A program may use at most 64 MiB of HBM per device.

v0:
```python
import math
import jax
import jax.numpy as jnp
from jax import lax
from jax.sharding import PartitionSpec as P

CT = 32


def shifted(value, axis, steps):
    count = lax.axis_size(axis)
    pairs = [(source, (source + steps) % count) for source in range(count)]
    return lax.ppermute(value, axis, pairs)


def add_block(totals, a_panel, b_all, stack_list, count_live, group_size):
    is_live = jnp.arange(group_size, dtype=jnp.int32) < count_live
    a_pick = (
        stack_list[0][:, None] == jnp.arange(a_panel.shape[0], dtype=jnp.int32)[None, :]
    ).astype(jnp.float32)
    b_pick = (
        stack_list[1][:, None] == jnp.arange(b_all.shape[0], dtype=jnp.int32)[None, :]
    ).astype(jnp.float32)
    c_place = (
        jnp.arange(totals.shape[0], dtype=jnp.int32)[:, None] == stack_list[2][None, :]
    ) & is_live[None, :]
    c_place = c_place.astype(jnp.float32)
    left_tiles = jnp.einsum(
        "gs,sij->gij",
        a_pick,
        a_panel,
        precision=lax.Precision.HIGHEST,
        preferred_element_type=jnp.float32,
    )
    right_tiles = jnp.einsum(
        "gs,sij->gij",
        b_pick,
        b_all,
        precision=lax.Precision.HIGHEST,
        preferred_element_type=jnp.float32,
    )
    products = jnp.einsum(
        "gij,gjk->gik",
        left_tiles,
        right_tiles,
        precision=lax.Precision.HIGHEST,
        preferred_element_type=jnp.float32,
    )
    return totals + jnp.einsum(
        "mg,gik->mik",
        c_place,
        products,
        precision=lax.Precision.HIGHEST,
        preferred_element_type=jnp.float32,
    )


def apply_panel(totals, a_panel, b_all, stack_list, count_live):
    entries = stack_list.shape[1]
    group_size = math.gcd(entries, 32)
    totals = add_block(totals, a_panel, b_all, stack_list, count_live, group_size)
    return totals


def body(a_tiles, b_tiles, pair_lists, stack_counts):
    tile_width = a_tiles.shape[3]
    col_count = lax.axis_size("col")
    own_column = lax.axis_index("col")
    gathered_b = lax.all_gather(b_tiles, "row", axis=0, tiled=True)
    b_all = gathered_b.reshape(-1, tile_width, tile_width)
    lists_all = pair_lists[0, 0]
    counts_all = stack_counts[0, 0]

    def visit(totals, a_panel, panel_index, keep_flag):
        stack_list = lax.dynamic_index_in_dim(lists_all, panel_index, 0, keepdims=False)
        count_live = (
            lax.dynamic_index_in_dim(counts_all, panel_index, 0, keepdims=False) * keep_flag
        )
        return apply_panel(totals, a_panel, b_all, stack_list, count_live)

    totals = jnp.zeros((CT, tile_width, tile_width), jnp.float32)
    own_panel = a_tiles[0, 0]
    totals = visit(totals, own_panel, own_column, 1)

    def next_stop(stop_index, loop_state):
        totals_in, moving = loop_state
        moving = shifted(moving, "col", 1)
        panel_index = (own_column - stop_index) % col_count
        return (visit(totals_in, moving, panel_index, 1), moving)

    totals, moving = lax.fori_loop(1, col_count, next_stop, (totals, own_panel))
    return totals[None, None]


def solution(mesh):
    return jax.shard_map(
        body,
        mesh=mesh,
        in_specs=(
            P("row", "col", None, None, None),
            P("row", "col", None, None, None),
            P("row", "col", None, None, None),
            P("row", "col", None),
        ),
        out_specs=P("row", "col", None, None, None),
        check_vma=False,
    )
```

profile of v0, /device:TPU:0, one launch (start us, length us, event | category | flops | bytes accessed | tf_op | source)
XLA Modules:
  0.0 401.2 jit_solution(11839348177748028509)
XLA Ops:
  12.1 71.7 %all-gather.2.cloned.1.call-done = f32[8,1,8,128,128]{4,3,2,1,0:T(8,128)} async-done(((f32[1,1,8,128,128]{4,3,2,1,0:T(8,128)}), f32[8,1,8,128,128]{4,3,2,1,0:T(8,128)}) %all-gather.2.cloned.1.call-update) | async-done | bytes 4194320 | tf_op jit(solution)/shard_map/all_gather | solution.py:69
  83.8 6.1 %fusion.23 = f32[32,128,128]{2,0,1:T(8,128)S(1)} fusion(f32[64,128,128]{2,1,0:T(8,128)} %bitcast.51, s32[32]{0:T(128)S(1)} %get-tuple-element.202), kind=kOutput, calls=%fused_computation.26 | convolution fusion | flops 402655232 | bytes 6291584 | tf_op jit(solution)/shard_map/gs,sij->gij/dot_general | solution.py:35
  89.9 4.6 %fusion.27 = f32[32,128,128]{2,1,0:T(8,128)S(1)} fusion(f32[32,128,128]{2,0,1:T(8,128)S(1)} %fusion.23, f32[32,128,128]{2,0,1:T(8,128)S(1)} %fusion.30), kind=kOutput, calls=%fused_computation.30 | convolution fusion | flops 805306368 | bytes 6291456 | tf_op jit(solution)/shard_map/gij,gjk->gik/dot_general | solution.py:42
  96.9 294.9 %while.17 = (s32[]{:T(128)}, f32[32,128,128]{2,0,1:T(8,128)S(1)}, f32[8,128,128]{2,1,0:T(8,128)S(1)}, s32[]{:T(128)}, s32[16,3,32]{2,1,0:T(4,128)S(1)}, /*index=...) while((s32[]{:T(128)}, f32[32,128,128]{2,0,1:T(8,128)S(1)}, ...), condition=%wide.region_1.2_spmd, body=%wide.region_0.1_spmd.sunk | while | flops 1460146432 | bytes 24643844 | solution.py:91
  98.4 6.1 %fusion.66 = f32[32,128,128]{2,0,1:T(8,128)S(1)} fusion(f32[64,128,128]{2,1,0:T(8,128)} %get-tuple-element.280, s32[32]{0:T(128)S(1)} %get-tuple-element.249), kind=kOutput, calls=%fused_computation.clone.1 | convolution fusion | flops 402655232 | bytes 6291584 | tf_op jit(solution)/shard_map/while/body/eval_jaxpr/gs,sij->gij/dot_general | solution.py:35
  104.5 3.4 collective-permute-done
  108.9 4.6 %fusion.68 = f32[32,128,128]{2,1,0:T(8,128)S(1)} fusion(f32[32,128,128]{2,0,1:T(8,128)S(1)} %fusion.66, f32[32,128,128]{2,0,1:T(8,128)S(1)} %fusion.67), kind=kOutput, calls=%fused_computation.4.clone.1 | convolution fusion | flops 805306368 | bytes 6291456 | tf_op jit(solution)/shard_map/while/body/eval_jaxpr/gij,gjk->gik/dot_general | solution.py:42
  118.1 6.1 %fusion.66 = f32[32,128,128]{2,0,1:T(8,128)S(1)} fusion(f32[64,128,128]{2,1,0:T(8,128)} %get-tuple-element.280, s32[32]{0:T(128)S(1)} %get-tuple-element.249), kind=kOutput, calls=%fused_computation.clone.1 | convolution fusion | flops 402655232 | bytes 6291584 | tf_op jit(solution)/shard_map/while/body/eval_jaxpr/gs,sij->gij/dot_general | solution.py:35
  124.2 3.4 collective-permute-done
  128.6 4.6 %fusion.68 = f32[32,128,128]{2,1,0:T(8,128)S(1)} fusion(f32[32,128,128]{2,0,1:T(8,128)S(1)} %fusion.66, f32[32,128,128]{2,0,1:T(8,128)S(1)} %fusion.67), kind=kOutput, calls=%fused_computation.4.clone.1 | convolution fusion | flops 805306368 | bytes 6291456 | tf_op jit(solution)/shard_map/while/body/eval_jaxpr/gij,gjk->gik/dot_general | solution.py:42
  137.7 6.1 %fusion.66 = f32[32,128,128]{2,0,1:T(8,128)S(1)} fusion(f32[64,128,128]{2,1,0:T(8,128)} %get-tuple-element.280, s32[32]{0:T(128)S(1)} %get-tuple-element.249), kind=kOutput, calls=%fused_computation.clone.1 | convolution fusion | flops 402655232 | bytes 6291584 | tf_op jit(solution)/shard_map/while/body/eval_jaxpr/gs,sij->gij/dot_general | solution.py:35
  143.8 3.4 collective-permute-done
  148.2 4.6 %fusion.68 = f32[32,128,128]{2,1,0:T(8,128)S(1)} fusion(f32[32,128,128]{2,0,1:T(8,128)S(1)} %fusion.66, f32[32,128,128]{2,0,1:T(8,128)S(1)} %fusion.67), kind=kOutput, calls=%fused_computation.4.clone.1 | convolution fusion | flops 805306368 | bytes 6291456 | tf_op jit(solution)/shard_map/while/body/eval_jaxpr/gij,gjk->gik/dot_general | solution.py:42
  157.4 6.1 %fusion.66 = f32[32,128,128]{2,0,1:T(8,128)S(1)} fusion(f32[64,128,128]{2,1,0:T(8,128)} %get-tuple-element.280, s32[32]{0:T(128)S(1)} %get-tuple-element.249), kind=kOutput, calls=%fused_computation.clone.1 | convolution fusion | flops 402655232 | bytes 6291584 | tf_op jit(solution)/shard_map/while/body/eval_jaxpr/gs,sij->gij/dot_general | solution.py:35
  163.5 3.4 collective-permute-done
  167.9 4.6 %fusion.68 = f32[32,128,128]{2,1,0:T(8,128)S(1)} fusion(f32[32,128,128]{2,0,1:T(8,128)S(1)} %fusion.66, f32[32,128,128]{2,0,1:T(8,128)S(1)} %fusion.67), kind=kOutput, calls=%fused_computation.4.clone.1 | convolution fusion | flops 805306368 | bytes 6291456 | tf_op jit(solution)/shard_map/while/body/eval_jaxpr/gij,gjk->gik/dot_general | solution.py:42
  177.0 6.1 %fusion.66 = f32[32,128,128]{2,0,1:T(8,128)S(1)} fusion(f32[64,128,128]{2,1,0:T(8,128)} %get-tuple-element.280, s32[32]{0:T(128)S(1)} %get-tuple-element.249), kind=kOutput, calls=%fused_computation.clone.1 | convolution fusion | flops 402655232 | bytes 6291584 | tf_op jit(solution)/shard_map/while/body/eval_jaxpr/gs,sij->gij/dot_general | solution.py:35
  183.1 3.4 collective-permute-done
  187.5 4.6 %fusion.68 = f32[32,128,128]{2,1,0:T(8,128)S(1)} fusion(f32[32,128,128]{2,0,1:T(8,128)S(1)} %fusion.66, f32[32,128,128]{2,0,1:T(8,128)S(1)} %fusion.67), kind=kOutput, calls=%fused_computation.4.clone.1 | convolution fusion | flops 805306368 | bytes 6291456 | tf_op jit(solution)/shard_map/while/body/eval_jaxpr/gij,gjk->gik/dot_general | solution.py:42
  196.7 6.1 %fusion.66 = f32[32,128,128]{2,0,1:T(8,128)S(1)} fusion(f32[64,128,128]{2,1,0:T(8,128)} %get-tuple-element.280, s32[32]{0:T(128)S(1)} %get-tuple-element.249), kind=kOutput, calls=%fused_computation.clone.1 | convolution fusion | flops 402655232 | bytes 6291584 | tf_op jit(solution)/shard_map/while/body/eval_jaxpr/gs,sij->gij/dot_general | solution.py:35
  202.7 3.4 collective-permute-done
  207.2 4.6 %fusion.68 = f32[32,128,128]{2,1,0:T(8,128)S(1)} fusion(f32[32,128,128]{2,0,1:T(8,128)S(1)} %fusion.66, f32[32,128,128]{2,0,1:T(8,128)S(1)} %fusion.67), kind=kOutput, calls=%fused_computation.4.clone.1 | convolution fusion | flops 805306368 | bytes 6291456 | tf_op jit(solution)/shard_map/while/body/eval_jaxpr/gij,gjk->gik/dot_general | solution.py:42
  216.3 6.1 %fusion.66 = f32[32,128,128]{2,0,1:T(8,128)S(1)} fusion(f32[64,128,128]{2,1,0:T(8,128)} %get-tuple-element.280, s32[32]{0:T(128)S(1)} %get-tuple-element.249), kind=kOutput, calls=%fused_computation.clone.1 | convolution fusion | flops 402655232 | bytes 6291584 | tf_op jit(solution)/shard_map/while/body/eval_jaxpr/gs,sij->gij/dot_general | solution.py:35
  222.4 3.4 collective-permute-done
  226.8 4.6 %fusion.68 = f32[32,128,128]{2,1,0:T(8,128)S(1)} fusion(f32[32,128,128]{2,0,1:T(8,128)S(1)} %fusion.66, f32[32,128,128]{2,0,1:T(8,128)S(1)} %fusion.67), kind=kOutput, calls=%fused_computation.4.clone.1 | convolution fusion | flops 805306368 | bytes 6291456 | tf_op jit(solution)/shard_map/while/body/eval_jaxpr/gij,gjk->gik/dot_general | solution.py:42
  236.0 6.1 %fusion.66 = f32[32,128,128]{2,0,1:T(8,128)S(1)} fusion(f32[64,128,128]{2,1,0:T(8,128)} %get-tuple-element.280, s32[32]{0:T(128)S(1)} %get-tuple-element.249), kind=kOutput, calls=%fused_computation.clone.1 | convolution fusion | flops 402655232 | bytes 6291584 | tf_op jit(solution)/shard_map/while/body/eval_jaxpr/gs,sij->gij/dot_general | solution.py:35
  242.0 3.4 collective-permute-done
  246.5 4.6 %fusion.68 = f32[32,128,128]{2,1,0:T(8,128)S(1)} fusion(f32[32,128,128]{2,0,1:T(8,128)S(1)} %fusion.66, f32[32,128,128]{2,0,1:T(8,128)S(1)} %fusion.67), kind=kOutput, calls=%fused_computation.4.clone.1 | convolution fusion | flops 805306368 | bytes 6291456 | tf_op jit(solution)/shard_map/while/body/eval_jaxpr/gij,gjk->gik/dot_general | solution.py:42
  255.6 6.1 %fusion.66 = f32[32,128,128]{2,0,1:T(8,128)S(1)} fusion(f32[64,128,128]{2,1,0:T(8,128)} %get-tuple-element.280, s32[32]{0:T(128)S(1)} %get-tuple-element.249), kind=kOutput, calls=%fused_computation.clone.1 | convolution fusion | flops 402655232 | bytes 6291584 | tf_op jit(solution)/shard_map/while/body/eval_jaxpr/gs,sij->gij/dot_general | solution.py:35
  261.7 3.4 collective-permute-done
  266.1 4.6 %fusion.68 = f32[32,128,128]{2,1,0:T(8,128)S(1)} fusion(f32[32,128,128]{2,0,1:T(8,128)S(1)} %fusion.66, f32[32,128,128]{2,0,1:T(8,128)S(1)} %fusion.67), kind=kOutput, calls=%fused_computation.4.clone.1 | convolution fusion | flops 805306368 | bytes 6291456 | tf_op jit(solution)/shard_map/while/body/eval_jaxpr/gij,gjk->gik/dot_general | solution.py:42
  275.3 6.1 %fusion.66 = f32[32,128,128]{2,0,1:T(8,128)S(1)} fusion(f32[64,128,128]{2,1,0:T(8,128)} %get-tuple-element.280, s32[32]{0:T(128)S(1)} %get-tuple-element.249), kind=kOutput, calls=%fused_computation.clone.1 | convolution fusion | flops 402655232 | bytes 6291584 | tf_op jit(solution)/shard_map/while/body/eval_jaxpr/gs,sij->gij/dot_general | solution.py:35
  281.3 3.4 collective-permute-done
  285.8 4.6 %fusion.68 = f32[32,128,128]{2,1,0:T(8,128)S(1)} fusion(f32[32,128,128]{2,0,1:T(8,128)S(1)} %fusion.66, f32[32,128,128]{2,0,1:T(8,128)S(1)} %fusion.67), kind=kOutput, calls=%fused_computation.4.clone.1 | convolution fusion | flops 805306368 | bytes 6291456 | tf_op jit(solution)/shard_map/while/body/eval_jaxpr/gij,gjk->gik/dot_general | solution.py:42
  294.9 6.1 %fusion.66 = f32[32,128,128]{2,0,1:T(8,128)S(1)} fusion(f32[64,128,128]{2,1,0:T(8,128)} %get-tuple-element.280, s32[32]{0:T(128)S(1)} %get-tuple-element.249), kind=kOutput, calls=%fused_computation.clone.1 | convolution fusion | flops 402655232 | bytes 6291584 | tf_op jit(solution)/shard_map/while/body/eval_jaxpr/gs,sij->gij/dot_general | solution.py:35
  301.0 3.4 collective-permute-done
  305.4 4.6 %fusion.68 = f32[32,128,128]{2,1,0:T(8,128)S(1)} fusion(f32[32,128,128]{2,0,1:T(8,128)S(1)} %fusion.66, f32[32,128,128]{2,0,1:T(8,128)S(1)} %fusion.67), kind=kOutput, calls=%fused_computation.4.clone.1 | convolution fusion | flops 805306368 | bytes 6291456 | tf_op jit(solution)/shard_map/while/body/eval_jaxpr/gij,gjk->gik/dot_general | solution.py:42
  314.6 6.1 %fusion.66 = f32[32,128,128]{2,0,1:T(8,128)S(1)} fusion(f32[64,128,128]{2,1,0:T(8,128)} %get-tuple-element.280, s32[32]{0:T(128)S(1)} %get-tuple-element.249), kind=kOutput, calls=%fused_computation.clone.1 | convolution fusion | flops 402655232 | bytes 6291584 | tf_op jit(solution)/shard_map/while/body/eval_jaxpr/gs,sij->gij/dot_general | solution.py:35
  320.6 3.4 collective-permute-done
  325.1 4.6 %fusion.68 = f32[32,128,128]{2,1,0:T(8,128)S(1)} fusion(f32[32,128,128]{2,0,1:T(8,128)S(1)} %fusion.66, f32[32,128,128]{2,0,1:T(8,128)S(1)} %fusion.67), kind=kOutput, calls=%fused_computation.4.clone.1 | convolution fusion | flops 805306368 | bytes 6291456 | tf_op jit(solution)/shard_map/while/body/eval_jaxpr/gij,gjk->gik/dot_general | solution.py:42
  334.2 6.1 %fusion.66 = f32[32,128,128]{2,0,1:T(8,128)S(1)} fusion(f32[64,128,128]{2,1,0:T(8,128)} %get-tuple-element.280, s32[32]{0:T(128)S(1)} %get-tuple-element.249), kind=kOutput, calls=%fused_computation.clone.1 | convolution fusion | flops 402655232 | bytes 6291584 | tf_op jit(solution)/shard_map/while/body/eval_jaxpr/gs,sij->gij/dot_general | solution.py:35
  340.3 3.4 collective-permute-done
  344.7 4.6 %fusion.68 = f32[32,128,128]{2,1,0:T(8,128)S(1)} fusion(f32[32,128,128]{2,0,1:T(8,128)S(1)} %fusion.66, f32[32,128,128]{2,0,1:T(8,128)S(1)} %fusion.67), kind=kOutput, calls=%fused_computation.4.clone.1 | convolution fusion | flops 805306368 | bytes 6291456 | tf_op jit(solution)/shard_map/while/body/eval_jaxpr/gij,gjk->gik/dot_general | solution.py:42
  353.8 6.1 %fusion.66 = f32[32,128,128]{2,0,1:T(8,128)S(1)} fusion(f32[64,128,128]{2,1,0:T(8,128)} %get-tuple-element.280, s32[32]{0:T(128)S(1)} %get-tuple-element.249), kind=kOutput, calls=%fused_computation.clone.1 | convolution fusion | flops 402655232 | bytes 6291584 | tf_op jit(solution)/shard_map/while/body/eval_jaxpr/gs,sij->gij/dot_general | solution.py:35
  364.4 4.6 %fusion.68 = f32[32,128,128]{2,1,0:T(8,128)S(1)} fusion(f32[32,128,128]{2,0,1:T(8,128)S(1)} %fusion.66, f32[32,128,128]{2,0,1:T(8,128)S(1)} %fusion.67), kind=kOutput, calls=%fused_computation.4.clone.1 | convolution fusion | flops 805306368 | bytes 6291456 | tf_op jit(solution)/shard_map/while/body/eval_jaxpr/gij,gjk->gik/dot_general | solution.py:42
  373.5 6.1 %fusion.66 = f32[32,128,128]{2,0,1:T(8,128)S(1)} fusion(f32[64,128,128]{2,1,0:T(8,128)} %get-tuple-element.280, s32[32]{0:T(128)S(1)} %get-tuple-element.249), kind=kOutput, calls=%fused_computation.clone.1 | convolution fusion | flops 402655232 | bytes 6291584 | tf_op jit(solution)/shard_map/while/body/eval_jaxpr/gs,sij->gij/dot_general | solution.py:35
  379.6 3.4 collective-permute-done
  384.0 4.6 %fusion.68 = f32[32,128,128]{2,1,0:T(8,128)S(1)} fusion(f32[32,128,128]{2,0,1:T(8,128)S(1)} %fusion.66, f32[32,128,128]{2,0,1:T(8,128)S(1)} %fusion.67), kind=kOutput, calls=%fused_computation.4.clone.1 | convolution fusion | flops 805306368 | bytes 6291456 | tf_op jit(solution)/shard_map/while/body/eval_jaxpr/gij,gjk->gik/dot_general | solution.py:42
  (133 shorter events, 97.2 us)
Async XLA Ops:
  6.5 77.3 %all-gather.2.cloned.1.call-start = ((), (), s32[]{:S(2)}) async-start(), calls=%async_computation | async-start | bytes 4718592 | tf_op jit(solution)/shard_map/all_gather | solution.py:69
  94.4 2.4 copy-start
  97.1 10.8 %collective-permute-start = (f32[8,128,128]{2,1,0:T(8,128)S(1)}, f32[8,128,128]{2,1,0:T(8,128)S(1)}, u32[]{:S(2)}, u32[]{:S(2)}) collective-permute-start(f32[8,128,128]{2,1,0:T(8,128)S(1)} %get-tuple-element.265), channel_id=1, source_target_pairs={{0,1},{1,2},{2,3},{3,4},{4,5},{5,6},{6,7},{7,8},{8,9},{9,10},{10,1... | collective-permute-start | bytes 1572872 | tf_op jit(solution)/shard_map/while/body/eval_jaxpr/ppermute | solution.py:13
  116.7 10.8 %collective-permute-start = (f32[8,128,128]{2,1,0:T(8,128)S(1)}, f32[8,128,128]{2,1,0:T(8,128)S(1)}, u32[]{:S(2)}, u32[]{:S(2)}) collective-permute-start(f32[8,128,128]{2,1,0:T(8,128)S(1)} %get-tuple-element.265), channel_id=1, source_target_pairs={{0,1},{1,2},{2,3},{3,4},{4,5},{5,6},{6,7},{7,8},{8,9},{9,10},{10,1... | collective-permute-start | bytes 1572872 | tf_op jit(solution)/shard_map/while/body/eval_jaxpr/ppermute | solution.py:13
  136.4 10.8 %collective-permute-start = (f32[8,128,128]{2,1,0:T(8,128)S(1)}, f32[8,128,128]{2,1,0:T(8,128)S(1)}, u32[]{:S(2)}, u32[]{:S(2)}) collective-permute-start(f32[8,128,128]{2,1,0:T(8,128)S(1)} %get-tuple-element.265), channel_id=1, source_target_pairs={{0,1},{1,2},{2,3},{3,4},{4,5},{5,6},{6,7},{7,8},{8,9},{9,10},{10,1... | collective-permute-start | bytes 1572872 | tf_op jit(solution)/shard_map/while/body/eval_jaxpr/ppermute | solution.py:13
  156.0 10.8 %collective-permute-start = (f32[8,128,128]{2,1,0:T(8,128)S(1)}, f32[8,128,128]{2,1,0:T(8,128)S(1)}, u32[]{:S(2)}, u32[]{:S(2)}) collective-permute-start(f32[8,128,128]{2,1,0:T(8,128)S(1)} %get-tuple-element.265), channel_id=1, source_target_pairs={{0,1},{1,2},{2,3},{3,4},{4,5},{5,6},{6,7},{7,8},{8,9},{9,10},{10,1... | collective-permute-start | bytes 1572872 | tf_op jit(solution)/shard_map/while/body/eval_jaxpr/ppermute | solution.py:13
  175.7 10.8 %collective-permute-start = (f32[8,128,128]{2,1,0:T(8,128)S(1)}, f32[8,128,128]{2,1,0:T(8,128)S(1)}, u32[]{:S(2)}, u32[]{:S(2)}) collective-permute-start(f32[8,128,128]{2,1,0:T(8,128)S(1)} %get-tuple-element.265), channel_id=1, source_target_pairs={{0,1},{1,2},{2,3},{3,4},{4,5},{5,6},{6,7},{7,8},{8,9},{9,10},{10,1... | collective-permute-start | bytes 1572872 | tf_op jit(solution)/shard_map/while/body/eval_jaxpr/ppermute | solution.py:13
  195.3 10.8 %collective-permute-start = (f32[8,128,128]{2,1,0:T(8,128)S(1)}, f32[8,128,128]{2,1,0:T(8,128)S(1)}, u32[]{:S(2)}, u32[]{:S(2)}) collective-permute-start(f32[8,128,128]{2,1,0:T(8,128)S(1)} %get-tuple-element.265), channel_id=1, source_target_pairs={{0,1},{1,2},{2,3},{3,4},{4,5},{5,6},{6,7},{7,8},{8,9},{9,10},{10,1... | collective-permute-start | bytes 1572872 | tf_op jit(solution)/shard_map/while/body/eval_jaxpr/ppermute | solution.py:13
  215.0 10.8 %collective-permute-start = (f32[8,128,128]{2,1,0:T(8,128)S(1)}, f32[8,128,128]{2,1,0:T(8,128)S(1)}, u32[]{:S(2)}, u32[]{:S(2)}) collective-permute-start(f32[8,128,128]{2,1,0:T(8,128)S(1)} %get-tuple-element.265), channel_id=1, source_target_pairs={{0,1},{1,2},{2,3},{3,4},{4,5},{5,6},{6,7},{7,8},{8,9},{9,10},{10,1... | collective-permute-start | bytes 1572872 | tf_op jit(solution)/shard_map/while/body/eval_jaxpr/ppermute | solution.py:13
  234.6 10.8 %collective-permute-start = (f32[8,128,128]{2,1,0:T(8,128)S(1)}, f32[8,128,128]{2,1,0:T(8,128)S(1)}, u32[]{:S(2)}, u32[]{:S(2)}) collective-permute-start(f32[8,128,128]{2,1,0:T(8,128)S(1)} %get-tuple-element.265), channel_id=1, source_target_pairs={{0,1},{1,2},{2,3},{3,4},{4,5},{5,6},{6,7},{7,8},{8,9},{9,10},{10,1... | collective-permute-start | bytes 1572872 | tf_op jit(solution)/shard_map/while/body/eval_jaxpr/ppermute | solution.py:13
  254.3 10.8 %collective-permute-start = (f32[8,128,128]{2,1,0:T(8,128)S(1)}, f32[8,128,128]{2,1,0:T(8,128)S(1)}, u32[]{:S(2)}, u32[]{:S(2)}) collective-permute-start(f32[8,128,128]{2,1,0:T(8,128)S(1)} %get-tuple-element.265), channel_id=1, source_target_pairs={{0,1},{1,2},{2,3},{3,4},{4,5},{5,6},{6,7},{7,8},{8,9},{9,10},{10,1... | collective-permute-start | bytes 1572872 | tf_op jit(solution)/shard_map/while/body/eval_jaxpr/ppermute | solution.py:13
  273.9 10.8 %collective-permute-start = (f32[8,128,128]{2,1,0:T(8,128)S(1)}, f32[8,128,128]{2,1,0:T(8,128)S(1)}, u32[]{:S(2)}, u32[]{:S(2)}) collective-permute-start(f32[8,128,128]{2,1,0:T(8,128)S(1)} %get-tuple-element.265), channel_id=1, source_target_pairs={{0,1},{1,2},{2,3},{3,4},{4,5},{5,6},{6,7},{7,8},{8,9},{9,10},{10,1... | collective-permute-start | bytes 1572872 | tf_op jit(solution)/shard_map/while/body/eval_jaxpr/ppermute | solution.py:13
  293.5 10.8 %collective-permute-start = (f32[8,128,128]{2,1,0:T(8,128)S(1)}, f32[8,128,128]{2,1,0:T(8,128)S(1)}, u32[]{:S(2)}, u32[]{:S(2)}) collective-permute-start(f32[8,128,128]{2,1,0:T(8,128)S(1)} %get-tuple-element.265), channel_id=1, source_target_pairs={{0,1},{1,2},{2,3},{3,4},{4,5},{5,6},{6,7},{7,8},{8,9},{9,10},{10,1... | collective-permute-start | bytes 1572872 | tf_op jit(solution)/shard_map/while/body/eval_jaxpr/ppermute | solution.py:13
  313.2 10.8 %collective-permute-start = (f32[8,128,128]{2,1,0:T(8,128)S(1)}, f32[8,128,128]{2,1,0:T(8,128)S(1)}, u32[]{:S(2)}, u32[]{:S(2)}) collective-permute-start(f32[8,128,128]{2,1,0:T(8,128)S(1)} %get-tuple-element.265), channel_id=1, source_target_pairs={{0,1},{1,2},{2,3},{3,4},{4,5},{5,6},{6,7},{7,8},{8,9},{9,10},{10,1... | collective-permute-start | bytes 1572872 | tf_op jit(solution)/shard_map/while/body/eval_jaxpr/ppermute | solution.py:13
  332.8 10.8 %collective-permute-start = (f32[8,128,128]{2,1,0:T(8,128)S(1)}, f32[8,128,128]{2,1,0:T(8,128)S(1)}, u32[]{:S(2)}, u32[]{:S(2)}) collective-permute-start(f32[8,128,128]{2,1,0:T(8,128)S(1)} %get-tuple-element.265), channel_id=1, source_target_pairs={{0,1},{1,2},{2,3},{3,4},{4,5},{5,6},{6,7},{7,8},{8,9},{9,10},{10,1... | collective-permute-start | bytes 1572872 | tf_op jit(solution)/shard_map/while/body/eval_jaxpr/ppermute | solution.py:13
  352.5 10.8 %collective-permute-start = (f32[8,128,128]{2,1,0:T(8,128)S(1)}, f32[8,128,128]{2,1,0:T(8,128)S(1)}, u32[]{:S(2)}, u32[]{:S(2)}) collective-permute-start(f32[8,128,128]{2,1,0:T(8,128)S(1)} %get-tuple-element.265), channel_id=1, source_target_pairs={{0,1},{1,2},{2,3},{3,4},{4,5},{5,6},{6,7},{7,8},{8,9},{9,10},{10,1... | collective-permute-start | bytes 1572872 | tf_op jit(solution)/shard_map/while/body/eval_jaxpr/ppermute | solution.py:13
  372.1 10.8 %collective-permute-start = (f32[8,128,128]{2,1,0:T(8,128)S(1)}, f32[8,128,128]{2,1,0:T(8,128)S(1)}, u32[]{:S(2)}, u32[]{:S(2)}) collective-permute-start(f32[8,128,128]{2,1,0:T(8,128)S(1)} %get-tuple-element.265), channel_id=1, source_target_pairs={{0,1},{1,2},{2,3},{3,4},{4,5},{5,6},{6,7},{7,8},{8,9},{9,10},{10,1... | collective-permute-start | bytes 1572872 | tf_op jit(solution)/shard_map/while/body/eval_jaxpr/ppermute | solution.py:13
Sparse Core Ops, SparseCore 0:
  9.7 74.0 all-gather.1
where the time goes:
time: 402 us; the launch traced here: 401 us
  matrix products  237 us (59%)
  waiting for transfers between devices  122 us (30%)
  local copies, waits for them, and re-layouts  16 us (4%)
  between operations  13.5 us (3%)
  other arithmetic  9.96 us (2%)
    dot_general x16, matrix products, add_block(): jnp.einsum('gs,sij->gij', b_pick, b_all, precision=lax.Precision.HIGHEST,...  97 us
    dot_general x16, matrix products, add_block(): jnp.einsum('gij,gjk->gik', left_tiles, right_tiles, precision=lax.Precisi...  73.2 us
    all_gather x1, waiting for transfers between devices, body(): gathered_b = lax.all_gather(b_tiles, 'row', axis=0, tiled=True)  71.7 us
    ppermute x15, waiting for transfers between devices, shifted(): return lax.ppermute(value, axis, pairs)  50.3 us
    dot_general x16, matrix products, add_block(): jnp.einsum('mg,gik->mik', c_place, products, precision=lax.Precision.HIGH...  49.5 us
    dot_general x16, matrix products, add_block(): jnp.einsum('gs,sij->gij', a_pick, a_panel, precision=lax.Precision.HIGHES...  17.2 us
    dynamic_slice x16, local copies, waits for them, and re-layouts, visit(): lax.dynamic_index_in_dim(counts_all, panel_index, 0, keepdims=False)  10.2 us
    lt x16, other arithmetic, add_block(): is_live = jnp.arange(group_size, dtype=jnp.int32) < count_live  9.96 us
  transfers between devices with their start and end apart: 16, of which 16 were waited for; matrix products, arithmetic and copies ran while one was open for 28% of the time, Pallas kernels for 0%

commit v1 on v0

--- a/solution.py
+++ b/solution.py
@@ -66,7 +66,10 @@
     tile_width = a_tiles.shape[3]
     col_count = lax.axis_size("col")
     own_column = lax.axis_index("col")
-    gathered_b = lax.all_gather(b_tiles, "row", axis=0, tiled=True)
+    link_series = lambda xx, chip_axis: jnp.concatenate(
+        lax.all_to_all(jnp.stack([xx] * lax.psum(1, chip_axis)), chip_axis, 0, 0), axis=0
+    )
+    gathered_b = link_series(b_tiles, "row")
     b_all = gathered_b.reshape(-1, tile_width, tile_width)
     lists_all = pair_lists[0, 0]
     counts_all = stack_counts[0, 0]

time: 402 us -> 373 us (0.928)
  waiting for transfers between devices: 122 us -> 96.8 us
  between operations: 13.5 us -> 0.08 us
  starting transfers between devices: 1.12 us -> 9.28 us
    all_gather x1 -> x0, waiting for transfers between devices: 71.7 us -> none  [body(): gathered_b = lax.all_gather(b_tiles, 'row', axis=0, tiled=True)]
    all_to_all x0 -> x1, waiting for transfers between devices: none -> 46.6 us  [body(): lax.all_to_all(jnp.stack([xx] * lax.psum(1, chip_axis)), chip_axis, 0, 0)]
    all_to_all x0 -> x1, starting transfers between devices: none -> 8.16 us  [body(): lax.all_to_all(jnp.stack([xx] * lax.psum(1, chip_axis)), chip_axis, 0, 0)]
  transfers between devices with their start and end apart: 16 -> 16, of which waited for: 16 -> 16; matrix products, arithmetic and copies ran while one was open for 28% -> 30% of each run, Pallas kernels for 0% -> 0%
where the time goes in v1:
time: 373 us; the launch traced here: 372 us
  matrix products  237 us (64%)
  waiting for transfers between devices  96.8 us (26%)
  local copies, waits for them, and re-layouts  17.8 us (5%)
  other arithmetic  9.78 us (3%)
  starting transfers between devices  9.28 us (2%)
    dot_general x16, matrix products, add_block(): jnp.einsum('gs,sij->gij', b_pick, b_all, precision=lax.Precision.HIGHEST,...  97 us
    dot_general x16, matrix products, add_block(): jnp.einsum('gij,gjk->gik', left_tiles, right_tiles, precision=lax.Precisi...  73.2 us
    ppermute x15, waiting for transfers between devices, shifted(): return lax.ppermute(value, axis, pairs)  50.2 us
    dot_general x16, matrix products, add_block(): jnp.einsum('mg,gik->mik', c_place, products, precision=lax.Precision.HIGH...  49.5 us
    all_to_all x1, waiting for transfers between devices, body(): lax.all_to_all(jnp.stack([xx] * lax.psum(1, chip_axis)), chip_axis, 0, 0)  46.6 us
    dot_general x16, matrix products, add_block(): jnp.einsum('gs,sij->gij', a_pick, a_panel, precision=lax.Precision.HIGHES...  17.2 us
    dynamic_slice x16, local copies, waits for them, and re-layouts, visit(): lax.dynamic_index_in_dim(counts_all, panel_index, 0, keepdims=False)  9.92 us
    lt x16, other arithmetic, add_block(): is_live = jnp.arange(group_size, dtype=jnp.int32) < count_live  9.78 us
  transfers between devices with their start and end apart: 16, of which 16 were waited for; matrix products, arithmetic and copies ran while one was open for 30% of the time, Pallas kernels for 0%

profile of v1, /device:TPU:0, one launch (start us, length us, event | category | flops | bytes accessed | tf_op | source)
XLA Modules:
  0.0 372.2 jit_solution(4315702813916285630)
XLA Ops:
  1.0 3.6 stack.2
  4.6 8.2 %all-to-all-start = ((f32[8,1,1,8,128,128]{5,4,3,2,1,0:T(8,128)}), f32[8,1,1,8,128,128]{5,4,3,2,1,0:T(8,128)}, u32[]{:S(2)}, u32[]{:S(2)}) async-start(f32[8,1,1,8,128,128]{5,4,3,2,1,0:T(8,128)} %stack.2), calls=%async_computation | async-start | bytes 8388608 | tf_op jit(solution)/shard_map/all_to_all | solution.py:70
  15.2 46.6 %all-to-all-done = f32[8,1,1,8,128,128]{5,4,3,2,1,0:T(8,128)} async-done(((f32[8,1,1,8,128,128]{5,4,3,2,1,0:T(8,128)}), f32[8,1,1,8,128,128]{5,4,3,2,1,0:T(8,128)}, u32[]{:S(2)}, u32[]{:S(2)}) %all-to-all-start) | async-done | bytes 4194336 | tf_op jit(solution)/shard_map/all_to_all | solution.py:70
  61.8 6.1 %fusion.23 = f32[32,128,128]{2,0,1:T(8,128)S(1)} fusion(f32[64,128,128]{2,1,0:T(8,128)} %bitcast.16, s32[32]{0:T(128)S(1)} %get-tuple-element.202), kind=kOutput, calls=%fused_computation.26 | convolution fusion | flops 402655232 | bytes 6291584 | tf_op jit(solution)/shard_map/gs,sij->gij/dot_general | solution.py:35
  67.8 4.6 %fusion.27 = f32[32,128,128]{2,1,0:T(8,128)S(1)} fusion(f32[32,128,128]{2,0,1:T(8,128)S(1)} %fusion.23, f32[32,128,128]{2,0,1:T(8,128)S(1)} %fusion.30), kind=kOutput, calls=%fused_computation.30 | convolution fusion | flops 805306368 | bytes 6291456 | tf_op jit(solution)/shard_map/gij,gjk->gik/dot_general | solution.py:42
  74.8 294.9 %while.17 = (s32[]{:T(128)}, f32[32,128,128]{2,0,1:T(8,128)S(1)}, f32[8,128,128]{2,1,0:T(8,128)S(1)}, s32[]{:T(128)}, s32[16,3,32]{2,1,0:T(4,128)S(1)}, /*index=...) while((s32[]{:T(128)}, f32[32,128,128]{2,0,1:T(8,128)S(1)}, ...), condition=%wide.region_1.2_spmd, body=%wide.region_0.1_spmd.sunk | while | flops 1460146432 | bytes 24643844 | solution.py:94
  76.4 6.1 %fusion.66 = f32[32,128,128]{2,0,1:T(8,128)S(1)} fusion(f32[64,128,128]{2,1,0:T(8,128)} %get-tuple-element.280, s32[32]{0:T(128)S(1)} %get-tuple-element.249), kind=kOutput, calls=%fused_computation.clone.1 | convolution fusion | flops 402655232 | bytes 6291584 | tf_op jit(solution)/shard_map/while/body/eval_jaxpr/gs,sij->gij/dot_general | solution.py:35
  86.9 4.6 %fusion.68 = f32[32,128,128]{2,1,0:T(8,128)S(1)} fusion(f32[32,128,128]{2,0,1:T(8,128)S(1)} %fusion.66, f32[32,128,128]{2,0,1:T(8,128)S(1)} %fusion.67), kind=kOutput, calls=%fused_computation.4.clone.1 | convolution fusion | flops 805306368 | bytes 6291456 | tf_op jit(solution)/shard_map/while/body/eval_jaxpr/gij,gjk->gik/dot_general | solution.py:42
  96.0 6.1 %fusion.66 = f32[32,128,128]{2,0,1:T(8,128)S(1)} fusion(f32[64,128,128]{2,1,0:T(8,128)} %get-tuple-element.280, s32[32]{0:T(128)S(1)} %get-tuple-element.249), kind=kOutput, calls=%fused_computation.clone.1 | convolution fusion | flops 402655232 | bytes 6291584 | tf_op jit(solution)/shard_map/while/body/eval_jaxpr/gs,sij->gij/dot_general | solution.py:35
  106.5 4.6 %fusion.68 = f32[32,128,128]{2,1,0:T(8,128)S(1)} fusion(f32[32,128,128]{2,0,1:T(8,128)S(1)} %fusion.66, f32[32,128,128]{2,0,1:T(8,128)S(1)} %fusion.67), kind=kOutput, calls=%fused_computation.4.clone.1 | convolution fusion | flops 805306368 | bytes 6291456 | tf_op jit(solution)/shard_map/while/body/eval_jaxpr/gij,gjk->gik/dot_general | solution.py:42
  115.7 6.1 %fusion.66 = f32[32,128,128]{2,0,1:T(8,128)S(1)} fusion(f32[64,128,128]{2,1,0:T(8,128)} %get-tuple-element.280, s32[32]{0:T(128)S(1)} %get-tuple-element.249), kind=kOutput, calls=%fused_computation.clone.1 | convolution fusion | flops 402655232 | bytes 6291584 | tf_op jit(solution)/shard_map/while/body/eval_jaxpr/gs,sij->gij/dot_general | solution.py:35
  121.7 3.3 collective-permute-done
  126.2 4.6 %fusion.68 = f32[32,128,128]{2,1,0:T(8,128)S(1)} fusion(f32[32,128,128]{2,0,1:T(8,128)S(1)} %fusion.66, f32[32,128,128]{2,0,1:T(8,128)S(1)} %fusion.67), kind=kOutput, calls=%fused_computation.4.clone.1 | convolution fusion | flops 805306368 | bytes 6291456 | tf_op jit(solution)/shard_map/while/body/eval_jaxpr/gij,gjk->gik/dot_general | solution.py:42
  135.3 6.1 %fusion.66 = f32[32,128,128]{2,0,1:T(8,128)S(1)} fusion(f32[64,128,128]{2,1,0:T(8,128)} %get-tuple-element.280, s32[32]{0:T(128)S(1)} %get-tuple-element.249), kind=kOutput, calls=%fused_computation.clone.1 | convolution fusion | flops 402655232 | bytes 6291584 | tf_op jit(solution)/shard_map/while/body/eval_jaxpr/gs,sij->gij/dot_general | solution.py:35
  141.4 3.3 collective-permute-done
  145.8 4.6 %fusion.68 = f32[32,128,128]{2,1,0:T(8,128)S(1)} fusion(f32[32,128,128]{2,0,1:T(8,128)S(1)} %fusion.66, f32[32,128,128]{2,0,1:T(8,128)S(1)} %fusion.67), kind=kOutput, calls=%fused_computation.4.clone.1 | convolution fusion | flops 805306368 | bytes 6291456 | tf_op jit(solution)/shard_map/while/body/eval_jaxpr/gij,gjk->gik/dot_general | solution.py:42
  155.0 6.1 %fusion.66 = f32[32,128,128]{2,0,1:T(8,128)S(1)} fusion(f32[64,128,128]{2,1,0:T(8,128)} %get-tuple-element.280, s32[32]{0:T(128)S(1)} %get-tuple-element.249), kind=kOutput, calls=%fused_computation.clone.1 | convolution fusion | flops 402655232 | bytes 6291584 | tf_op jit(solution)/shard_map/while/body/eval_jaxpr/gs,sij->gij/dot_general | solution.py:35
  161.0 3.3 collective-permute-done
  165.5 4.6 %fusion.68 = f32[32,128,128]{2,1,0:T(8,128)S(1)} fusion(f32[32,128,128]{2,0,1:T(8,128)S(1)} %fusion.66, f32[32,128,128]{2,0,1:T(8,128)S(1)} %fusion.67), kind=kOutput, calls=%fused_computation.4.clone.1 | convolution fusion | flops 805306368 | bytes 6291456 | tf_op jit(solution)/shard_map/while/body/eval_jaxpr/gij,gjk->gik/dot_general | solution.py:42
  174.6 6.1 %fusion.66 = f32[32,128,128]{2,0,1:T(8,128)S(1)} fusion(f32[64,128,128]{2,1,0:T(8,128)} %get-tuple-element.280, s32[32]{0:T(128)S(1)} %get-tuple-element.249), kind=kOutput, calls=%fused_computation.clone.1 | convolution fusion | flops 402655232 | bytes 6291584 | tf_op jit(solution)/shard_map/while/body/eval_jaxpr/gs,sij->gij/dot_general | solution.py:35
  180.7 3.3 collective-permute-done
  185.1 4.6 %fusion.68 = f32[32,128,128]{2,1,0:T(8,128)S(1)} fusion(f32[32,128,128]{2,0,1:T(8,128)S(1)} %fusion.66, f32[32,128,128]{2,0,1:T(8,128)S(1)} %fusion.67), kind=kOutput, calls=%fused_computation.4.clone.1 | convolution fusion | flops 805306368 | bytes 6291456 | tf_op jit(solution)/shard_map/while/body/eval_jaxpr/gij,gjk->gik/dot_general | solution.py:42
  194.3 6.1 %fusion.66 = f32[32,128,128]{2,0,1:T(8,128)S(1)} fusion(f32[64,128,128]{2,1,0:T(8,128)} %get-tuple-element.280, s32[32]{0:T(128)S(1)} %get-tuple-element.249), kind=kOutput, calls=%fused_computation.clone.1 | convolution fusion | flops 402655232 | bytes 6291584 | tf_op jit(solution)/shard_map/while/body/eval_jaxpr/gs,sij->gij/dot_general | solution.py:35
  200.3 3.3 collective-permute-done
  204.8 4.6 %fusion.68 = f32[32,128,128]{2,1,0:T(8,128)S(1)} fusion(f32[32,128,128]{2,0,1:T(8,128)S(1)} %fusion.66, f32[32,128,128]{2,0,1:T(8,128)S(1)} %fusion.67), kind=kOutput, calls=%fused_computation.4.clone.1 | convolution fusion | flops 805306368 | bytes 6291456 | tf_op jit(solution)/shard_map/while/body/eval_jaxpr/gij,gjk->gik/dot_general | solution.py:42
  213.9 6.1 %fusion.66 = f32[32,128,128]{2,0,1:T(8,128)S(1)} fusion(f32[64,128,128]{2,1,0:T(8,128)} %get-tuple-element.280, s32[32]{0:T(128)S(1)} %get-tuple-element.249), kind=kOutput, calls=%fused_computation.clone.1 | convolution fusion | flops 402655232 | bytes 6291584 | tf_op jit(solution)/shard_map/while/body/eval_jaxpr/gs,sij->gij/dot_general | solution.py:35
  220.0 3.3 collective-permute-done
  224.4 4.6 %fusion.68 = f32[32,128,128]{2,1,0:T(8,128)S(1)} fusion(f32[32,128,128]{2,0,1:T(8,128)S(1)} %fusion.66, f32[32,128,128]{2,0,1:T(8,128)S(1)} %fusion.67), kind=kOutput, calls=%fused_computation.4.clone.1 | convolution fusion | flops 805306368 | bytes 6291456 | tf_op jit(solution)/shard_map/while/body/eval_jaxpr/gij,gjk->gik/dot_general | solution.py:42
  233.6 6.1 %fusion.66 = f32[32,128,128]{2,0,1:T(8,128)S(1)} fusion(f32[64,128,128]{2,1,0:T(8,128)} %get-tuple-element.280, s32[32]{0:T(128)S(1)} %get-tuple-element.249), kind=kOutput, calls=%fused_computation.clone.1 | convolution fusion | flops 402655232 | bytes 6291584 | tf_op jit(solution)/shard_map/while/body/eval_jaxpr/gs,sij->gij/dot_general | solution.py:35
  239.6 3.3 collective-permute-done
  244.0 4.6 %fusion.68 = f32[32,128,128]{2,1,0:T(8,128)S(1)} fusion(f32[32,128,128]{2,0,1:T(8,128)S(1)} %fusion.66, f32[32,128,128]{2,0,1:T(8,128)S(1)} %fusion.67), kind=kOutput, calls=%fused_computation.4.clone.1 | convolution fusion | flops 805306368 | bytes 6291456 | tf_op jit(solution)/shard_map/while/body/eval_jaxpr/gij,gjk->gik/dot_general | solution.py:42
  253.2 6.1 %fusion.66 = f32[32,128,128]{2,0,1:T(8,128)S(1)} fusion(f32[64,128,128]{2,1,0:T(8,128)} %get-tuple-element.280, s32[32]{0:T(128)S(1)} %get-tuple-element.249), kind=kOutput, calls=%fused_computation.clone.1 | convolution fusion | flops 402655232 | bytes 6291584 | tf_op jit(solution)/shard_map/while/body/eval_jaxpr/gs,sij->gij/dot_general | solution.py:35
  259.3 3.3 collective-permute-done
  263.7 4.6 %fusion.68 = f32[32,128,128]{2,1,0:T(8,128)S(1)} fusion(f32[32,128,128]{2,0,1:T(8,128)S(1)} %fusion.66, f32[32,128,128]{2,0,1:T(8,128)S(1)} %fusion.67), kind=kOutput, calls=%fused_computation.4.clone.1 | convolution fusion | flops 805306368 | bytes 6291456 | tf_op jit(solution)/shard_map/while/body/eval_jaxpr/gij,gjk->gik/dot_general | solution.py:42
  272.8 6.1 %fusion.66 = f32[32,128,128]{2,0,1:T(8,128)S(1)} fusion(f32[64,128,128]{2,1,0:T(8,128)} %get-tuple-element.280, s32[32]{0:T(128)S(1)} %get-tuple-element.249), kind=kOutput, calls=%fused_computation.clone.1 | convolution fusion | flops 402655232 | bytes 6291584 | tf_op jit(solution)/shard_map/while/body/eval_jaxpr/gs,sij->gij/dot_general | solution.py:35
  283.3 4.6 %fusion.68 = f32[32,128,128]{2,1,0:T(8,128)S(1)} fusion(f32[32,128,128]{2,0,1:T(8,128)S(1)} %fusion.66, f32[32,128,128]{2,0,1:T(8,128)S(1)} %fusion.67), kind=kOutput, calls=%fused_computation.4.clone.1 | convolution fusion | flops 805306368 | bytes 6291456 | tf_op jit(solution)/shard_map/while/body/eval_jaxpr/gij,gjk->gik/dot_general | solution.py:42
  292.5 6.1 %fusion.66 = f32[32,128,128]{2,0,1:T(8,128)S(1)} fusion(f32[64,128,128]{2,1,0:T(8,128)} %get-tuple-element.280, s32[32]{0:T(128)S(1)} %get-tuple-element.249), kind=kOutput, calls=%fused_computation.clone.1 | convolution fusion | flops 402655232 | bytes 6291584 | tf_op jit(solution)/shard_map/while/body/eval_jaxpr/gs,sij->gij/dot_general | solution.py:35
  298.6 3.3 collective-permute-done
  303.0 4.6 %fusion.68 = f32[32,128,128]{2,1,0:T(8,128)S(1)} fusion(f32[32,128,128]{2,0,1:T(8,128)S(1)} %fusion.66, f32[32,128,128]{2,0,1:T(8,128)S(1)} %fusion.67), kind=kOutput, calls=%fused_computation.4.clone.1 | convolution fusion | flops 805306368 | bytes 6291456 | tf_op jit(solution)/shard_map/while/body/eval_jaxpr/gij,gjk->gik/dot_general | solution.py:42
  312.1 6.1 %fusion.66 = f32[32,128,128]{2,0,1:T(8,128)S(1)} fusion(f32[64,128,128]{2,1,0:T(8,128)} %get-tuple-element.280, s32[32]{0:T(128)S(1)} %get-tuple-element.249), kind=kOutput, calls=%fused_computation.clone.1 | convolution fusion | flops 402655232 | bytes 6291584 | tf_op jit(solution)/shard_map/while/body/eval_jaxpr/gs,sij->gij/dot_general | solution.py:35
  318.2 3.3 collective-permute-done
  322.6 4.6 %fusion.68 = f32[32,128,128]{2,1,0:T(8,128)S(1)} fusion(f32[32,128,128]{2,0,1:T(8,128)S(1)} %fusion.66, f32[32,128,128]{2,0,1:T(8,128)S(1)} %fusion.67), kind=kOutput, calls=%fused_computation.4.clone.1 | convolution fusion | flops 805306368 | bytes 6291456 | tf_op jit(solution)/shard_map/while/body/eval_jaxpr/gij,gjk->gik/dot_general | solution.py:42
  331.8 6.1 %fusion.66 = f32[32,128,128]{2,0,1:T(8,128)S(1)} fusion(f32[64,128,128]{2,1,0:T(8,128)} %get-tuple-element.280, s32[32]{0:T(128)S(1)} %get-tuple-element.249), kind=kOutput, calls=%fused_computation.clone.1 | convolution fusion | flops 402655232 | bytes 6291584 | tf_op jit(solution)/shard_map/while/body/eval_jaxpr/gs,sij->gij/dot_general | solution.py:35
  337.9 3.3 collective-permute-done
  342.3 4.6 %fusion.68 = f32[32,128,128]{2,1,0:T(8,128)S(1)} fusion(f32[32,128,128]{2,0,1:T(8,128)S(1)} %fusion.66, f32[32,128,128]{2,0,1:T(8,128)S(1)} %fusion.67), kind=kOutput, calls=%fused_computation.4.clone.1 | convolution fusion | flops 805306368 | bytes 6291456 | tf_op jit(solution)/shard_map/while/body/eval_jaxpr/gij,gjk->gik/dot_general | solution.py:42
  351.4 6.1 %fusion.66 = f32[32,128,128]{2,0,1:T(8,128)S(1)} fusion(f32[64,128,128]{2,1,0:T(8,128)} %get-tuple-element.280, s32[32]{0:T(128)S(1)} %get-tuple-element.249), kind=kOutput, calls=%fused_computation.clone.1 | convolution fusion | flops 402655232 | bytes 6291584 | tf_op jit(solution)/shard_map/while/body/eval_jaxpr/gs,sij->gij/dot_general | solution.py:35
  357.5 3.3 collective-permute-done
  361.9 4.6 %fusion.68 = f32[32,128,128]{2,1,0:T(8,128)S(1)} fusion(f32[32,128,128]{2,0,1:T(8,128)S(1)} %fusion.66, f32[32,128,128]{2,0,1:T(8,128)S(1)} %fusion.67), kind=kOutput, calls=%fused_computation.4.clone.1 | convolution fusion | flops 805306368 | bytes 6291456 | tf_op jit(solution)/shard_map/while/body/eval_jaxpr/gij,gjk->gik/dot_general | solution.py:42
  (135 shorter events, 101.8 us)
Async XLA Ops:
  4.6 8.2 %copy-start = (s32[1,1,16,3,32]{4,2,3,1,0:T(8,128)S(1)}, s32[1,1,16,3,32]{4,2,3,1,0:T(8,128)}, u32[]{:S(2)}) copy-start(s32[1,1,16,3,32]{4,2,3,1,0:T(8,128)} %param.8) | copy-start | bytes 18436
  4.6 8.2 %copy-start.1 = (s32[1,1,16]{2,1,0:T(1,128)S(1)}, s32[1,1,16]{2,1,0:T(1,128)}, u32[]{:S(2)}) copy-start(s32[1,1,16]{2,1,0:T(1,128)} %param.9) | copy-start | bytes 196
  4.6 57.1 %all-to-all-start = ((f32[8,1,1,8,128,128]{5,4,3,2,1,0:T(8,128)}), f32[8,1,1,8,128,128]{5,4,3,2,1,0:T(8,128)}, u32[]{:S(2)}, u32[]{:S(2)}) async-start(f32[8,1,1,8,128,128]{5,4,3,2,1,0:T(8,128)} %stack.2), calls=%async_computation | async-start | bytes 8388608 | tf_op jit(solution)/shard_map/all_to_all | solution.py:70
  75.0 10.8 %collective-permute-start = (f32[8,128,128]{2,1,0:T(8,128)S(1)}, f32[8,128,128]{2,1,0:T(8,128)S(1)}, u32[]{:S(2)}, u32[]{:S(2)}) collective-permute-start(f32[8,128,128]{2,1,0:T(8,128)S(1)} %get-tuple-element.265), channel_id=1, source_target_pairs={{0,1},{1,2},{2,3},{3,4},{4,5},{5,6},{6,7},{7,8},{8,9},{9,10},{10,1... | collective-permute-start | bytes 1572872 | tf_op jit(solution)/shard_map/while/body/eval_jaxpr/ppermute | solution.py:13
  94.7 10.8 %collective-permute-start = (f32[8,128,128]{2,1,0:T(8,128)S(1)}, f32[8,128,128]{2,1,0:T(8,128)S(1)}, u32[]{:S(2)}, u32[]{:S(2)}) collective-permute-start(f32[8,128,128]{2,1,0:T(8,128)S(1)} %get-tuple-element.265), channel_id=1, source_target_pairs={{0,1},{1,2},{2,3},{3,4},{4,5},{5,6},{6,7},{7,8},{8,9},{9,10},{10,1... | collective-permute-start | bytes 1572872 | tf_op jit(solution)/shard_map/while/body/eval_jaxpr/ppermute | solution.py:13
  114.3 10.8 %collective-permute-start = (f32[8,128,128]{2,1,0:T(8,128)S(1)}, f32[8,128,128]{2,1,0:T(8,128)S(1)}, u32[]{:S(2)}, u32[]{:S(2)}) collective-permute-start(f32[8,128,128]{2,1,0:T(8,128)S(1)} %get-tuple-element.265), channel_id=1, source_target_pairs={{0,1},{1,2},{2,3},{3,4},{4,5},{5,6},{6,7},{7,8},{8,9},{9,10},{10,1... | collective-permute-start | bytes 1572872 | tf_op jit(solution)/shard_map/while/body/eval_jaxpr/ppermute | solution.py:13
  134.0 10.8 %collective-permute-start = (f32[8,128,128]{2,1,0:T(8,128)S(1)}, f32[8,128,128]{2,1,0:T(8,128)S(1)}, u32[]{:S(2)}, u32[]{:S(2)}) collective-permute-start(f32[8,128,128]{2,1,0:T(8,128)S(1)} %get-tuple-element.265), channel_id=1, source_target_pairs={{0,1},{1,2},{2,3},{3,4},{4,5},{5,6},{6,7},{7,8},{8,9},{9,10},{10,1... | collective-permute-start | bytes 1572872 | tf_op jit(solution)/shard_map/while/body/eval_jaxpr/ppermute | solution.py:13
  153.6 10.8 %collective-permute-start = (f32[8,128,128]{2,1,0:T(8,128)S(1)}, f32[8,128,128]{2,1,0:T(8,128)S(1)}, u32[]{:S(2)}, u32[]{:S(2)}) collective-permute-start(f32[8,128,128]{2,1,0:T(8,128)S(1)} %get-tuple-element.265), channel_id=1, source_target_pairs={{0,1},{1,2},{2,3},{3,4},{4,5},{5,6},{6,7},{7,8},{8,9},{9,10},{10,1... | collective-permute-start | bytes 1572872 | tf_op jit(solution)/shard_map/while/body/eval_jaxpr/ppermute | solution.py:13
  173.2 10.8 %collective-permute-start = (f32[8,128,128]{2,1,0:T(8,128)S(1)}, f32[8,128,128]{2,1,0:T(8,128)S(1)}, u32[]{:S(2)}, u32[]{:S(2)}) collective-permute-start(f32[8,128,128]{2,1,0:T(8,128)S(1)} %get-tuple-element.265), channel_id=1, source_target_pairs={{0,1},{1,2},{2,3},{3,4},{4,5},{5,6},{6,7},{7,8},{8,9},{9,10},{10,1... | collective-permute-start | bytes 1572872 | tf_op jit(solution)/shard_map/while/body/eval_jaxpr/ppermute | solution.py:13
  192.9 10.8 %collective-permute-start = (f32[8,128,128]{2,1,0:T(8,128)S(1)}, f32[8,128,128]{2,1,0:T(8,128)S(1)}, u32[]{:S(2)}, u32[]{:S(2)}) collective-permute-start(f32[8,128,128]{2,1,0:T(8,128)S(1)} %get-tuple-element.265), channel_id=1, source_target_pairs={{0,1},{1,2},{2,3},{3,4},{4,5},{5,6},{6,7},{7,8},{8,9},{9,10},{10,1... | collective-permute-start | bytes 1572872 | tf_op jit(solution)/shard_map/while/body/eval_jaxpr/ppermute | solution.py:13
  212.5 10.8 %collective-permute-start = (f32[8,128,128]{2,1,0:T(8,128)S(1)}, f32[8,128,128]{2,1,0:T(8,128)S(1)}, u32[]{:S(2)}, u32[]{:S(2)}) collective-permute-start(f32[8,128,128]{2,1,0:T(8,128)S(1)} %get-tuple-element.265), channel_id=1, source_target_pairs={{0,1},{1,2},{2,3},{3,4},{4,5},{5,6},{6,7},{7,8},{8,9},{9,10},{10,1... | collective-permute-start | bytes 1572872 | tf_op jit(solution)/shard_map/while/body/eval_jaxpr/ppermute | solution.py:13
  232.2 10.8 %collective-permute-start = (f32[8,128,128]{2,1,0:T(8,128)S(1)}, f32[8,128,128]{2,1,0:T(8,128)S(1)}, u32[]{:S(2)}, u32[]{:S(2)}) collective-permute-start(f32[8,128,128]{2,1,0:T(8,128)S(1)} %get-tuple-element.265), channel_id=1, source_target_pairs={{0,1},{1,2},{2,3},{3,4},{4,5},{5,6},{6,7},{7,8},{8,9},{9,10},{10,1... | collective-permute-start | bytes 1572872 | tf_op jit(solution)/shard_map/while/body/eval_jaxpr/ppermute | solution.py:13
  251.8 10.8 %collective-permute-start = (f32[8,128,128]{2,1,0:T(8,128)S(1)}, f32[8,128,128]{2,1,0:T(8,128)S(1)}, u32[]{:S(2)}, u32[]{:S(2)}) collective-permute-start(f32[8,128,128]{2,1,0:T(8,128)S(1)} %get-tuple-element.265), channel_id=1, source_target_pairs={{0,1},{1,2},{2,3},{3,4},{4,5},{5,6},{6,7},{7,8},{8,9},{9,10},{10,1... | collective-permute-start | bytes 1572872 | tf_op jit(solution)/shard_map/while/body/eval_jaxpr/ppermute | solution.py:13
  271.5 10.8 %collective-permute-start = (f32[8,128,128]{2,1,0:T(8,128)S(1)}, f32[8,128,128]{2,1,0:T(8,128)S(1)}, u32[]{:S(2)}, u32[]{:S(2)}) collective-permute-start(f32[8,128,128]{2,1,0:T(8,128)S(1)} %get-tuple-element.265), channel_id=1, source_target_pairs={{0,1},{1,2},{2,3},{3,4},{4,5},{5,6},{6,7},{7,8},{8,9},{9,10},{10,1... | collective-permute-start | bytes 1572872 | tf_op jit(solution)/shard_map/while/body/eval_jaxpr/ppermute | solution.py:13
  291.1 10.8 %collective-permute-start = (f32[8,128,128]{2,1,0:T(8,128)S(1)}, f32[8,128,128]{2,1,0:T(8,128)S(1)}, u32[]{:S(2)}, u32[]{:S(2)}) collective-permute-start(f32[8,128,128]{2,1,0:T(8,128)S(1)} %get-tuple-element.265), channel_id=1, source_target_pairs={{0,1},{1,2},{2,3},{3,4},{4,5},{5,6},{6,7},{7,8},{8,9},{9,10},{10,1... | collective-permute-start | bytes 1572872 | tf_op jit(solution)/shard_map/while/body/eval_jaxpr/ppermute | solution.py:13
  310.8 10.8 %collective-permute-start = (f32[8,128,128]{2,1,0:T(8,128)S(1)}, f32[8,128,128]{2,1,0:T(8,128)S(1)}, u32[]{:S(2)}, u32[]{:S(2)}) collective-permute-start(f32[8,128,128]{2,1,0:T(8,128)S(1)} %get-tuple-element.265), channel_id=1, source_target_pairs={{0,1},{1,2},{2,3},{3,4},{4,5},{5,6},{6,7},{7,8},{8,9},{9,10},{10,1... | collective-permute-start | bytes 1572872 | tf_op jit(solution)/shard_map/while/body/eval_jaxpr/ppermute | solution.py:13
  330.4 10.8 %collective-permute-start = (f32[8,128,128]{2,1,0:T(8,128)S(1)}, f32[8,128,128]{2,1,0:T(8,128)S(1)}, u32[]{:S(2)}, u32[]{:S(2)}) collective-permute-start(f32[8,128,128]{2,1,0:T(8,128)S(1)} %get-tuple-element.265), channel_id=1, source_target_pairs={{0,1},{1,2},{2,3},{3,4},{4,5},{5,6},{6,7},{7,8},{8,9},{9,10},{10,1... | collective-permute-start | bytes 1572872 | tf_op jit(solution)/shard_map/while/body/eval_jaxpr/ppermute | solution.py:13
  350.1 10.8 %collective-permute-start = (f32[8,128,128]{2,1,0:T(8,128)S(1)}, f32[8,128,128]{2,1,0:T(8,128)S(1)}, u32[]{:S(2)}, u32[]{:S(2)}) collective-permute-start(f32[8,128,128]{2,1,0:T(8,128)S(1)} %get-tuple-element.265), channel_id=1, source_target_pairs={{0,1},{1,2},{2,3},{3,4},{4,5},{5,6},{6,7},{7,8},{8,9},{9,10},{10,1... | collective-permute-start | bytes 1572872 | tf_op jit(solution)/shard_map/while/body/eval_jaxpr/ppermute | solution.py:13
